TPU v7x, 128 devices: a whole 4x4x4 slice. The times are simulated.
128 devices in a mesh: tok: 4 (over y), seq: 16 (over z, x), kv: 2 (over core).
Axes of the slice: x: 4, y: 4, z: 4, core: 2. Of those that a mesh axis runs over, the one named last changes fastest.
Arguments:
- token_ids: int32 [64, 4], replicated, may hold values from 0 to 32767
- request_order: int32 [64], replicated, may hold values from 0 to 63, each once
- cache_lengths: int32 [64], replicated, may hold values from 1 to 16384, 524288 in all
- embed_table: bfloat16 [32768, 2048], P(('tok', 'kv'), 'seq'), may hold values from -3 to 3
- attn_gain: bfloat16 [2048], replicated, may hold values from 0.099609375 to 1.8984375
- proj_query: bfloat16 [2048, 2048], P(None, ('tok', 'kv')), may hold values from -0.125 to 0.125
- proj_kv: bfloat16 [2048, 8, 128], P(None, ('tok', 'kv')), may hold values from -0.125 to 0.125
- kv_cache: bfloat16 [64, 16384, 8, 128], P(None, 'seq', ('tok', 'kv')), may hold values from -125 to 125, as said below
- proj_out: bfloat16 [2048, 2048], P(('tok', 'kv'), 'seq'), may hold values from -0.25 to 0.25
- mlp_gain: bfloat16 [2048], replicated, may hold values from 0.099609375 to 1.8984375
- proj_gate: bfloat16 [2048, 8192], P(None, 'seq'), may hold values from -0.125 to 0.125
- proj_up: bfloat16 [2048, 8192], P(None, 'seq'), may hold values from -0.125 to 0.125
- proj_down: bfloat16 [8192, 2048], P('seq'), may hold values from -0.0625 to 0.0625
Outputs:
- hidden_out: bfloat16 [64, 4, 2048], P(('tok', 'kv'), None, 'seq')
Inputs may be any that keep to these rules, and one draw needn't show every extreme that they name: `request_order`: every request stands in exactly one slot. `cache_lengths`: the lengths sum to 524288 and the largest equals 16384. `kv_cache`: cached keys are already rotated to their positions.
All inputs are finite; a program needn't handle non-finite values.
Results may differ from a plain program's by a relative error of at most 0.018.
The roundings to bfloat16 on the way count: a program that leaves them out, or rounds other values in their place, can miss the bound.
Values may be sent and summed in bfloat16 or wider, within the bound.
A program may use at most 128 MiB of HBM per device.

v0:
```python
import jax
import jax.numpy as jnp
from jax import lax
from jax.sharding import PartitionSpec as P

EPSILON = 1e-05
ROPE_BASE = 1000000.0
FLOOR_SCORE = -1e30


def combined_all(value, axis, join):
    pieces = jax.tree.map(lambda part: lax.all_gather(part, axis), value)
    head = jax.tree.map(lambda part: part[0], pieces)
    tail = jax.tree.map(lambda part: part[1:], pieces)
    so_far, _ = lax.scan(lambda so_far, share: (join(so_far, share), None), head, tail)
    return so_far


def rotate(vector, position):
    half_dim = vector.shape[-1] // 2
    frequency = ROPE_BASE ** (-(jnp.arange(half_dim, dtype=jnp.float32) * 2.0 / vector.shape[-1]))
    angles = position[..., None] * frequency
    cosine = jnp.cos(angles)
    sine_part = jnp.sin(angles)
    front_half = vector[..., :half_dim]
    back_half = vector[..., half_dim:]
    return jnp.concatenate(
        [front_half * cosine - back_half * sine_part, back_half * cosine + front_half * sine_part],
        axis=-1,
    )


def combine(earlier, later):
    peak_a, mass_a, accum_a = earlier
    peak_b, mass_b, accum_b = later
    highest = jnp.maximum(peak_a, peak_b)
    factor_a = jnp.exp(peak_a - highest)
    factor_b = jnp.exp(peak_b - highest)
    return (
        highest,
        mass_a * factor_a + mass_b * factor_b,
        accum_a * factor_a[..., None] + accum_b * factor_b[..., None],
    )


def per_device(
    token_ids,
    request_order,
    cache_lengths,
    embed_table,
    attn_gain,
    proj_query,
    proj_kv,
    kv_cache,
    proj_out,
    mlp_gain,
    proj_gate,
    proj_up,
    proj_down,
):
    n_req, n_steps = token_ids.shape
    width = proj_query.shape[0]
    head_dim = kv_cache.shape[-1] // 2
    group_heads = proj_query.shape[1] // head_dim
    ctx_dev = kv_cache.shape[1]
    columns = embed_table.shape[1]
    vocab_rows = embed_table.shape[0]
    scale = head_dim ** (-0.5)
    owners = lax.axis_size("tok") * lax.axis_size("kv")
    owner_index = lax.axis_index("tok") * lax.axis_size("kv") + lax.axis_index("kv")
    seq_rank = lax.axis_index("seq")
    offset = token_ids.reshape(-1) - owner_index * vocab_rows
    inside = (offset >= 0) & (offset < vocab_rows)
    picked = jnp.take(embed_table, jnp.clip(offset, 0, vocab_rows - 1), axis=0)
    partial_x = jnp.where(inside[:, None], picked.astype(jnp.float32), 0.0)
    local_x = lax.psum(partial_x.astype(jnp.bfloat16), ("tok", "kv"))
    kv_flat = proj_kv.reshape(width, -1)
    full_x = lax.all_gather(local_x, "seq", axis=1, tiled=True)
    widened = full_x.astype(jnp.float32)
    square_mean = jnp.mean(widened * widened, axis=1)
    scaled = (widened * attn_gain.astype(jnp.float32)).astype(jnp.bfloat16)
    q_raw = jnp.dot(scaled, proj_query, preferred_element_type=jnp.float32)
    kv_raw = jnp.dot(scaled, kv_flat, preferred_element_type=jnp.float32)
    inv_norm = lax.rsqrt(square_mean + EPSILON)[:, None]
    q_scaled = (q_raw * inv_norm).reshape(n_req, n_steps, group_heads, head_dim)
    kv_scaled = (kv_raw * inv_norm).reshape(n_req, n_steps, 2 * head_dim)
    position = (cache_lengths[:, None] + jnp.arange(n_steps, dtype=jnp.int32)[None, :]).astype(
        jnp.float32
    )
    query = rotate(q_scaled, position[:, :, None]).astype(jnp.bfloat16)
    new_keys = rotate(kv_scaled[..., :head_dim], position).astype(jnp.bfloat16)
    new_values = kv_scaled[..., head_dim:].astype(jnp.bfloat16)
    cache_rows = kv_cache[:, :, 0, :]
    key_part = cache_rows[..., :head_dim]
    value_part = cache_rows[..., head_dim:]
    scores = (
        jnp.einsum("rjgd,rpd->rjgp", query, key_part, preferred_element_type=jnp.float32) * scale
    )
    places = seq_rank * ctx_dev + jnp.arange(ctx_dev, dtype=jnp.int32)
    is_live = (places[None, :] < cache_lengths[:, None])[:, None, None, :]
    masked = jnp.where(is_live, scores, FLOOR_SCORE)
    block_peak = jnp.max(masked, axis=-1)
    block_weight = jnp.where(is_live, jnp.exp(masked - block_peak[..., None]), 0.0).astype(
        jnp.bfloat16
    )
    block_mass = jnp.sum(block_weight.astype(jnp.float32), axis=-1)
    block_accum = jnp.einsum(
        "rjgp,rpd->rjgd", block_weight, value_part, preferred_element_type=jnp.float32
    )
    peak_all, mass_all, accum_all = combined_all(
        (block_peak, block_mass, block_accum), "seq", combine
    )
    fresh_scores = (
        jnp.einsum("rjgd,rkd->rjgk", query, new_keys, preferred_element_type=jnp.float32) * scale
    )
    causal = (jnp.arange(n_steps)[:, None] >= jnp.arange(n_steps)[None, :])[None, :, None, :]
    fresh_masked = jnp.where(causal, fresh_scores, FLOOR_SCORE)
    fresh_peak = jnp.max(fresh_masked, axis=-1)
    fresh_weight = jnp.where(causal, jnp.exp(fresh_masked - fresh_peak[..., None]), 0.0).astype(
        jnp.bfloat16
    )
    fresh_mass = jnp.sum(fresh_weight.astype(jnp.float32), axis=-1)
    fresh_accum = jnp.einsum(
        "rjgk,rkd->rjgd", fresh_weight, new_values, preferred_element_type=jnp.float32
    )
    highest = jnp.maximum(peak_all, fresh_peak)
    cache_factor = jnp.exp(peak_all - highest)
    fresh_factor = jnp.exp(fresh_peak - highest)
    numer = accum_all * cache_factor[..., None] + fresh_accum * fresh_factor[..., None]
    denom = mass_all * cache_factor + fresh_mass * fresh_factor
    attended = (
        (numer / denom[..., None])
        .astype(jnp.bfloat16)
        .reshape(n_req, n_steps, group_heads * head_dim)
    )
    slot_rows = attended[request_order].reshape(n_req * n_steps, group_heads * head_dim)
    per_owner = n_req // owners
    attn_part = lax.psum_scatter(
        jnp.dot(slot_rows, proj_out, preferred_element_type=jnp.float32),
        ("tok", "kv"),
        scatter_dimension=0,
        tiled=True,
    )
    my_requests = lax.dynamic_slice_in_dim(request_order, owner_index * per_owner, per_owner)
    own_x = local_x.reshape(n_req, n_steps, columns)[my_requests].reshape(
        per_owner * n_steps, columns
    )
    mid = (own_x.astype(jnp.float32) + attn_part).astype(jnp.bfloat16)
    piece_wide = lax.all_gather(mid, "seq", axis=1, tiled=True).astype(jnp.float32)
    gain_part = mlp_gain.astype(jnp.float32)
    piece_scaled = (piece_wide * gain_part).astype(jnp.bfloat16)
    gate_acc = jnp.dot(piece_scaled, proj_gate, preferred_element_type=jnp.float32)
    up_acc = jnp.dot(piece_scaled, proj_up, preferred_element_type=jnp.float32)
    square_total = jnp.sum(piece_wide * piece_wide, axis=1)
    inv_mlp = lax.rsqrt(square_total / width + EPSILON)[:, None]
    hidden = (jax.nn.silu(gate_acc * inv_mlp) * (up_acc * inv_mlp)).astype(jnp.bfloat16)
    down_terms = jnp.dot(hidden, proj_down, preferred_element_type=jnp.float32)
    mlp_part = lax.psum_scatter(down_terms, "seq", scatter_dimension=1, tiled=True)
    result = (mid.astype(jnp.float32) + mlp_part).astype(jnp.bfloat16)
    return result.reshape(per_owner, n_steps, columns)


def solution(mesh):
    placed = (
        P(),
        P(),
        P(),
        P(("tok", "kv"), "seq"),
        P(),
        P(None, ("tok", "kv")),
        P(None, ("tok", "kv"), None),
        P(None, "seq", ("tok", "kv"), None),
        P(("tok", "kv"), "seq"),
        P(),
        P(None, "seq"),
        P(None, "seq"),
        P("seq", None),
    )
    return jax.shard_map(
        per_device,
        mesh=mesh,
        in_specs=placed,
        out_specs=P(("tok", "kv"), None, "seq"),
        check_vma=False,
    )
```

profile of v0, /device:TPU:0, one launch (start us, length us, event | category | flops | bytes accessed | tf_op | source)
XLA Modules:
  0.0 429.6 jit_solution(7146980658867892863)
XLA Ops:
  6.5 0.8 compare_and_fusion.1
  8.7 2.1 gather_fusion
  11.6 61.3 %all-reduce.2.cloned.1.call-done = bf16[256,128]{1,0:T(8,128)(2,1)} async-done(((bf16[256,128]{1,0:T(8,128)(2,1)}), bf16[256,128]{1,0:T(8,128)(2,1)}) %all-reduce.2.cloned.1.call-update) | async-done | bytes 65552 | tf_op jit(solution)/shard_map/psum | solution.py:76
  73.6 22.1 %copy.87 = bf16[64,1024,1,128]{1,3,0,2:T(8,128)(2,1)} copy(bf16[64,1024,1,128]{3,1,2,0:T(8,128)(2,1)} %param.22) | data formatting | bytes 33554432 | tf_op args[7]
  96.5 21.2 %all-gather.6.cloned.1.call-done = bf16[256,2048]{1,0:T(8,128)(2,1)} async-done(((bf16[256,128]{1,0:T(8,128)(2,1)}), bf16[256,2048]{1,0:T(8,128)(2,1)}) %all-gather.6.cloned.1.call-update) | async-done | bytes 1048592 | tf_op jit(solution)/shard_map/all_gather | solution.py:78
  117.7 1.5 fusion.7
  119.2 2.0 convolution_multiply_fusion.1
  121.4 1.8 convolution_multiply_fusion.2
  123.5 1.0 multiply_cosine_fusion
  125.2 6.2 %fusion.5 = (f32[64,4,4]{2,1,0:T(4,128)S(1)}, f32[64,4,4,1024]{3,2,1,0:T(4,128)S(1)}) fusion(pred[64,1024]{1,0:T(8,128)(4,1)} %broadcast_compare_fusion, bf16[64,1024,128]{1,2,0:T(8,128)(2,1)} %bitcast.67, bf16[64,4,4,32]{3,2,1,0:T(4,128)(2,1)S(1)} %get-tuple-element.101, bf16[64,4,4,32]{3,2,1,0:T(4,128)(2,1)S(1)} %get-tuple-element.100), kind=kOutput, calls=%fused_computation.18 | convolution fusion | flops 137624576 | bytes 12783616 | tf_op jit(solution)/shard_map/rjgd,rpd->rjgp/dot_general | solution.py:97
  131.4 3.7 convert_reduce_fusion
  135.1 6.8 %fusion.3 = f32[64,4,4,64]{3,2,1,0:T(4,128)} fusion(bf16[64,4,4,1024]{3,2,1,0:T(4,128)(2,1)S(1)} %get-tuple-element.99, bf16[64,1024,128]{1,2,0:T(8,128)(2,1)} %bitcast.68), kind=kOutput, calls=%fused_computation.12 | convolution fusion | flops 134217728 | bytes 10747904 | tf_op jit(solution)/shard_map/rjgp,rpd->rjgd/dot_general | solution.py:107
  142.7 30.8 %all-gather.1 = f32[1024,4,4]{2,1,0:T(4,128)S(1)} all-gather(f32[64,4,4]{2,1,0:T(4,128)S(1)} %get-tuple-element.98), channel_id=3, replica_groups=mesh['tok'=4,'seq'=16,'kv'=2] {'seq'}, dimensions={0}, use_global_device_ids=true | all-gather | bytes 69632 | tf_op jit(solution)/shard_map/all_gather | solution.py:12
  173.5 1.4 slice.76
  174.9 32.0 %all-gather = f32[1024,4,4]{2,1,0:T(4,128)S(1)} all-gather(f32[64,4,4]{2,1,0:T(4,128)S(1)} %get-tuple-element.110), channel_id=2, replica_groups=mesh['tok'=4,'seq'=16,'kv'=2] {'seq'}, dimensions={0}, use_global_device_ids=true | all-gather | bytes 69632 | tf_op jit(solution)/shard_map/all_gather | solution.py:12
  206.9 1.4 slice.75
  209.1 3.3 fusion.36
  213.6 1.0 copy.102
  214.6 2.7 copy.93
  217.4 2.2 copy.92
  219.6 5.8 %all-gather.8.cloned.1.call-done = f32[1024,4,4,64]{3,2,1,0:T(4,128)} async-done(((f32[64,4,4,64]{3,2,1,0:T(4,128)}), f32[1024,4,4,64]{3,2,1,0:T(4,128)}) %all-gather.8.cloned.1.call-update) | async-done | bytes 4194320 | tf_op jit(solution)/shard_map/all_gather | solution.py:12
  225.3 7.7 %slice.77 = f32[960,4,4,64]{3,2,1,0:T(4,128)} slice(f32[1024,4,4,64]{3,2,1,0:T(4,128)} %all-gather.8.cloned.1.call-done), slice={[64:1024], [0:4], [0:4], [0:64]} | slice | bytes 7864320 | tf_op jit(solution)/shard_map/slice | solution.py:14
  233.1 53.9 %while.14 = (s32[]{:T(128)}, f32[64,4,4]{0,2,1:T(4,128)S(1)}, f32[64,4,4]{0,2,1:T(4,128)S(1)}, f32[64,4,4,64]{3,2,1,0:T(4,128)S(1)}, f32[15,64,4,4]{1,3,2,0:T(4,...) while((s32[]{:T(128)}, f32[64,4,4]{0,2,1:T(4,128)S(1)}, ...), condition=%wide.region_5.6_spmd, body=%wide.region_4.5_spmd.sunk | while | flops 202754 | bytes 843877 | solution.py:15
  234.1 2.6 fusion.54
  237.7 2.6 fusion.54
  241.3 2.6 fusion.54
  244.9 2.6 fusion.54
  248.5 2.6 fusion.54
  252.1 2.6 fusion.54
  255.7 2.6 fusion.54
  259.2 2.6 fusion.54
  262.8 2.6 fusion.54
  266.4 2.6 fusion.54
  270.0 2.6 fusion.54
  273.6 2.6 fusion.54
  277.2 2.6 fusion.54
  280.8 2.6 fusion.54
  284.4 2.6 fusion.54
  288.7 2.0 fusion.10
  290.9 0.8 gather_fusion.2
  291.8 0.8 fusion.41
  292.8 1.4 gather_fusion.1
  294.2 28.3 %reduce-scatter.3.cloned.1.call-done = f32[32,128]{1,0:T(8,128)} async-done(((f32[256,128]{1,0:T(8,128)}), f32[32,128]{1,0:T(8,128)}) %reduce-scatter.3.cloned.1.call-update) | async-done | bytes 16400 | tf_op jit(solution)/shard_map/reduce_scatter | solution.py:138
  323.3 23.9 %all_gather.31 = bf16[32,2048]{1,0:T(8,128)(2,1)S(1)} all-gather(bf16[32,128]{1,0:T(8,128)(2,1)S(1)} %fusion.32), channel_id=1, replica_groups=mesh['tok'=4,'seq'=16,'kv'=2] {'seq'}, dimensions={1}, use_global_device_ids=true | all-gather | bytes 139264 | tf_op jit(solution)/shard_map/all_gather | solution.py:149
  347.3 2.0 convolution_multiply_fusion.4
  349.4 3.2 fusion.13
  352.6 69.2 %reduce-scatter.5.cloned.1.call-done = f32[32,128]{1,0:T(8,128)} async-done(((f32[32,2048]{1,0:T(8,128)}), f32[32,128]{1,0:T(8,128)}) %reduce-scatter.5.cloned.1.call-update) | async-done | bytes 16400 | tf_op jit(solution)/shard_map/reduce_scatter | solution.py:158
  421.8 1.3 add_convert_fusion.2
  (126 shorter events, 25.5 us)
Async XLA Ops:
  6.5 342.8 %copy-start = (bf16[512,2048]{1,0:T(8,128)(2,1)S(1)}, bf16[512,2048]{1,0:T(8,128)(2,1)}, u32[]{:S(2)}) copy-start(bf16[512,2048]{1,0:T(8,128)(2,1)} %param.27) | copy-start | bytes 6291460
  6.5 66.3 %all-reduce.2.cloned.1.call-start = ((), (), s32[]{:S(2)}) async-start(), calls=%async_computation.2 | async-start | bytes 131072 | tf_op jit(solution)/shard_map/psum | solution.py:76
  11.5 106.1 %all-gather.6.cloned.1.call-start = ((), (), s32[]{:S(2)}) async-start(), calls=%async_computation.3 | async-start | bytes 1114112 | tf_op jit(solution)/shard_map/all_gather | solution.py:78
  72.9 152.4 %all-gather.8.cloned.1.call-start = ((), (), s32[]{:S(2)}) async-start(), calls=%async_computation.6 | async-start | bytes 8912896 | tf_op jit(solution)/shard_map/all_gather | solution.py:12
  73.6 22.1 %copy-start.7 = (s32[64]{0:T(128)S(1)}, s32[64]{0:T(128)}, u32[]{:S(2)}) copy-start(s32[64]{0:T(128)} %param.17) | copy-start | bytes 772
  125.2 6.2 %copy-start.1 = (pred[64,1024]{1,0:T(8,128)(4,1)S(1)}, pred[64,1024]{1,0:T(8,128)(4,1)}, u32[]{:S(2)}) copy-start(pred[64,1024]{1,0:T(8,128)(4,1)} %broadcast_compare_fusion) | copy-start | bytes 196612
  135.1 6.9 %copy-start.9 = (s32[64]{0:T(128)S(1)}, s32[64]{0:T(128)}, u32[]{:S(2)}) copy-start(s32[64]{0:T(128)} %param.16) | copy-start | bytes 772
  142.0 180.5 %reduce-scatter.3.cloned.1.call-start = ((), (), s32[]{:S(2)}) async-start(), calls=%async_computation.4 | async-start | bytes 147456 | tf_op jit(solution)/shard_map/reduce_scatter | solution.py:138
  142.1 70.6 %copy-start.8 = (pred[4,4]{1,0:T(4,128)(4,1)}, pred[4,4]{1,0:T(4,128)(4,1)S(1)}, u32[]{:S(2)}) copy-start(pred[4,4]{1,0:T(4,128)(4,1)S(1)} %iota_compare_fusion) | copy-start | bytes 52
  174.9 33.4 %copy-start.3 = (bf16[64,4,32]{0,2,1:T(8,128)(2,1)S(1)}, bf16[64,4,32]{0,2,1:T(8,128)(2,1)}, u32[]{:S(2)}) copy-start(bf16[64,4,32]{0,2,1:T(8,128)(2,1)} %get-tuple-element.108) | copy-start | bytes 49156
  174.9 33.4 %copy-start.4 = (bf16[64,4,32]{0,2,1:T(8,128)(2,1)S(1)}, bf16[64,4,32]{0,2,1:T(8,128)(2,1)}, u32[]{:S(2)}) copy-start(bf16[64,4,32]{0,2,1:T(8,128)(2,1)} %get-tuple-element.109) | copy-start | bytes 49156
  225.3 7.7 %slice-start = ((f32[1024,4,4,64]{3,2,1,0:T(4,128)}), f32[64,4,4,64]{3,2,1,0:T(4,128)S(1)}, s32[]{:S(2)}) async-start(f32[1024,4,4,64]{3,2,1,0:T(4,128)} %all-gather.8.cloned.1.call-done), calls=%async_computation.7 | async-start | bytes 1048576 | tf_op jit(solution)/shard_map/slice | solution.py:13
  233.1 55.7 %copy-start.2 = (bf16[64,4,4,4]{3,2,1,0:T(4,128)(2,1)S(1)}, bf16[64,4,4,4]{3,2,1,0:T(4,128)(2,1)}, u32[]{:S(2)}) copy-start(bf16[64,4,4,4]{3,2,1,0:T(4,128)(2,1)} %copy.102) | copy-start | bytes 24580
  288.7 3.1 copy-start.5
  288.7 4.0 copy-start.6
  288.7 4.0 copy-start.10
  292.6 129.1 %reduce-scatter.5.cloned.1.call-start = ((), (), s32[]{:S(2)}) async-start(), calls=%async_computation.5 | async-start | bytes 278528 | tf_op jit(solution)/shard_map/reduce_scatter | solution.py:158
Sparse Core Ops, SparseCore 0:
  11.7 61.1 all-reduce.1
  75.2 42.4 all-gather.5
  142.1 83.1 all-gather.7
  292.8 29.7 reduce-scatter.2
  352.7 68.9 reduce-scatter.4
where the time goes:
time: 432 us; the launch traced here: 430 us
  waiting for transfers between devices  186 us (43%)
  blocking collectives  86.6 us (20%)
  other arithmetic  63.8 us (15%)
  local copies, waits for them, and re-layouts  51.2 us (12%)
  matrix products  28.1 us (7%)
  between operations  13.4 us (3%)
    reduce_scatter x1, waiting for transfers between devices, per_device(): lax.psum_scatter(down_terms, 'seq', scatter_dimension=1, tiled=True)  69.2 us
    all_gather x2, blocking collectives, combined_all(): pieces = jax.tree.map(lambda part: lax.all_gather(part, axis), value)  62.8 us
    psum x1, waiting for transfers between devices, per_device(): local_x = lax.psum(partial_x.astype(jnp.bfloat16), ('tok', 'kv'))  61.3 us
    add x15, other arithmetic, combine(): accum_a * factor_a[..., None] + accum_b * factor_b[..., None]  38.7 us
    reduce_scatter x1, waiting for transfers between devices, per_device(): lax.psum_scatter(jnp.dot(slot_rows, proj_out, preferred_element_type=jnp....  28.3 us
    all_gather x1, blocking collectives, per_device(): lax.all_gather(mid, 'seq', axis=1, tiled=True).astype(jnp.float32)  23.9 us
    unnamed x25, local copies, waits for them, and re-layouts  22.3 us
    all_gather x1, waiting for transfers between devices, per_device(): full_x = lax.all_gather(local_x, 'seq', axis=1, tiled=True)  21.2 us
  transfers between devices with their start and end apart: 5, of which 5 were waited for; matrix products, arithmetic and copies ran while one was open for 9% of the time, Pallas kernels for 0%

commit v1 on v0

--- a/solution.py
+++ b/solution.py
@@ -73,7 +73,7 @@
     inside = (offset >= 0) & (offset < vocab_rows)
     picked = jnp.take(embed_table, jnp.clip(offset, 0, vocab_rows - 1), axis=0)
     partial_x = jnp.where(inside[:, None], picked.astype(jnp.float32), 0.0)
-    local_x = lax.psum(partial_x.astype(jnp.bfloat16), ("tok", "kv"))
+    local_x = jnp.sum(lax.all_gather(partial_x.astype(jnp.bfloat16), ("tok", "kv")), axis=0)
     kv_flat = proj_kv.reshape(width, -1)
     full_x = lax.all_gather(local_x, "seq", axis=1, tiled=True)
     widened = full_x.astype(jnp.float32)

time: 432 us -> 385 us (0.89)
  waiting for transfers between devices: 186 us -> 125 us
  blocking collectives: 86.6 us -> 100 us
    psum x1 -> x0, waiting for transfers between devices: 61.3 us -> none  [per_device(): local_x = lax.psum(partial_x.astype(jnp.bfloat16), ('tok', 'kv'))]
    all_gather x0 -> x1, blocking collectives: none -> 13.7 us  [per_device(): lax.all_gather(partial_x.astype(jnp.bfloat16), ('tok', 'kv'))]
  transfers between devices with their start and end apart: 5 -> 4, of which waited for: 5 -> 4; matrix products, arithmetic and copies ran while one was open for 9% -> 10% of each run, Pallas kernels for 0% -> 0%
where the time goes in v1:
time: 385 us; the launch traced here: 382 us
  waiting for transfers between devices  125 us (32%)
  blocking collectives  100 us (26%)
  other arithmetic  64 us (17%)
  local copies, waits for them, and re-layouts  51.5 us (13%)
  matrix products  28.1 us (7%)
  between operations  13.4 us (3%)
    reduce_scatter x1, waiting for transfers between devices, per_device(): lax.psum_scatter(down_terms, 'seq', scatter_dimension=1, tiled=True)  69 us
    all_gather x2, blocking collectives, combined_all(): pieces = jax.tree.map(lambda part: lax.all_gather(part, axis), value)  62.8 us
    add x15, other arithmetic, combine(): accum_a * factor_a[..., None] + accum_b * factor_b[..., None]  38.7 us
    reduce_scatter x1, waiting for transfers between devices, per_device(): lax.psum_scatter(jnp.dot(slot_rows, proj_out, preferred_element_type=jnp....  28.3 us
    all_gather x1, blocking collectives, per_device(): lax.all_gather(mid, 'seq', axis=1, tiled=True).astype(jnp.float32)  23.8 us
    unnamed x25, local copies, waits for them, and re-layouts  22.6 us
    all_gather x1, waiting for transfers between devices, per_device(): full_x = lax.all_gather(local_x, 'seq', axis=1, tiled=True)  21.5 us
    all_gather x1, blocking collectives, per_device(): lax.all_gather(partial_x.astype(jnp.bfloat16), ('tok', 'kv'))  13.7 us
  transfers between devices with their start and end apart: 4, of which 4 were waited for; matrix products, arithmetic and copies ran while one was open for 10% of the time, Pallas kernels for 0%

profile of v1, /device:TPU:0, one launch (start us, length us, event | category | flops | bytes accessed | tf_op | source)
XLA Modules:
  0.0 382.4 jit_solution(11328825159960691946)
XLA Ops:
  6.5 0.8 compare_and_fusion.1
  8.7 2.1 gather_fusion
  10.9 13.7 %all_gather.28 = bf16[8,256,128]{2,1,0:T(8,128)(2,1)S(1)} all-gather(bf16[1,256,128]{2,1,0:T(8,128)(2,1)S(1)} %select_convert_fusion.1), channel_id=1, replica_groups=mesh['tok'=4,'seq'=16,'kv'=2] {'tok','kv'}, dimensions={0}, use_global_device_ids=true | all-gather | bytes 589824 | tf_op jit(solution)/shard_map/all_gather | solution.py:76
  26.1 22.4 %copy.103 = bf16[64,1024,1,128]{1,3,0,2:T(8,128)(2,1)} copy(bf16[64,1024,1,128]{3,1,2,0:T(8,128)(2,1)} %param.22) | data formatting | bytes 33554432 | tf_op args[7]
  49.2 21.5 %all-gather.6.cloned.1.call-done = bf16[256,2048]{1,0:T(8,128)(2,1)} async-done(((bf16[256,128]{1,0:T(8,128)(2,1)}), bf16[256,2048]{1,0:T(8,128)(2,1)}) %all-gather.6.cloned.1.call-update) | async-done | bytes 1048592 | tf_op jit(solution)/shard_map/all_gather | solution.py:78
  70.7 1.5 fusion.7
  72.2 2.0 convolution_multiply_fusion.1
  74.4 1.8 convolution_multiply_fusion.2
  76.5 1.0 multiply_cosine_fusion
  78.2 6.1 %fusion.5 = (f32[64,4,4]{2,1,0:T(4,128)S(1)}, f32[64,4,4,1024]{3,2,1,0:T(4,128)S(1)}) fusion(pred[64,1024]{1,0:T(8,128)(4,1)} %broadcast_compare_fusion, bf16[64,1024,128]{1,2,0:T(8,128)(2,1)} %bitcast.71, bf16[64,4,4,32]{3,2,1,0:T(4,128)(2,1)S(1)} %get-tuple-element.108, bf16[64,4,4,32]{3,2,1,0:T(4,128)(2,1)S(1)} %get-tuple-element.107), kind=kOutput, calls=%fused_computation.18 | convolution fusion | flops 137624576 | bytes 12783616 | tf_op jit(solution)/shard_map/rjgd,rpd->rjgp/dot_general | solution.py:97
  84.4 3.7 convert_reduce_fusion
  88.1 6.8 %fusion.3 = f32[64,4,4,64]{3,2,1,0:T(4,128)} fusion(bf16[64,4,4,1024]{3,2,1,0:T(4,128)(2,1)S(1)} %get-tuple-element.106, bf16[64,1024,128]{1,2,0:T(8,128)(2,1)} %bitcast.72), kind=kOutput, calls=%fused_computation.12 | convolution fusion | flops 134217728 | bytes 10747904 | tf_op jit(solution)/shard_map/rjgp,rpd->rjgd/dot_general | solution.py:107
  95.7 30.8 %all-gather.1 = f32[1024,4,4]{2,1,0:T(4,128)S(1)} all-gather(f32[64,4,4]{2,1,0:T(4,128)S(1)} %get-tuple-element.105), channel_id=3, replica_groups=mesh['tok'=4,'seq'=16,'kv'=2] {'seq'}, dimensions={0}, use_global_device_ids=true | all-gather | bytes 69632 | tf_op jit(solution)/shard_map/all_gather | solution.py:12
  126.5 1.4 slice.76
  127.9 32.0 %all-gather = f32[1024,4,4]{2,1,0:T(4,128)S(1)} all-gather(f32[64,4,4]{2,1,0:T(4,128)S(1)} %get-tuple-element.117), channel_id=2, replica_groups=mesh['tok'=4,'seq'=16,'kv'=2] {'seq'}, dimensions={0}, use_global_device_ids=true | all-gather | bytes 69632 | tf_op jit(solution)/shard_map/all_gather | solution.py:12
  159.9 1.5 slice.75
  162.1 3.3 fusion.36
  166.7 1.0 copy.118
  167.7 2.7 copy.109
  170.5 2.2 copy.108
  172.6 5.7 %all-gather.8.cloned.1.call-done = f32[1024,4,4,64]{3,2,1,0:T(4,128)} async-done(((f32[64,4,4,64]{3,2,1,0:T(4,128)}), f32[1024,4,4,64]{3,2,1,0:T(4,128)}) %all-gather.8.cloned.1.call-update) | async-done | bytes 4194320 | tf_op jit(solution)/shard_map/all_gather | solution.py:12
  178.3 7.7 %slice.77 = f32[960,4,4,64]{3,2,1,0:T(4,128)} slice(f32[1024,4,4,64]{3,2,1,0:T(4,128)} %all-gather.8.cloned.1.call-done), slice={[64:1024], [0:4], [0:4], [0:64]} | slice | bytes 7864320 | tf_op jit(solution)/shard_map/slice | solution.py:14
  186.1 53.9 %while.14 = (s32[]{:T(128)}, f32[64,4,4]{0,2,1:T(4,128)S(1)}, f32[64,4,4]{0,2,1:T(4,128)S(1)}, f32[64,4,4,64]{3,2,1,0:T(4,128)S(1)}, f32[15,64,4,4]{1,3,2,0:T(4,...) while((s32[]{:T(128)}, f32[64,4,4]{0,2,1:T(4,128)S(1)}, ...), condition=%wide.region_5.6_spmd, body=%wide.region_4.5_spmd.sunk | while | flops 202754 | bytes 843877 | solution.py:15
  187.1 2.6 fusion.54
  190.7 2.6 fusion.54
  194.3 2.6 fusion.54
  197.9 2.6 fusion.54
  201.5 2.6 fusion.54
  205.1 2.6 fusion.54
  208.7 2.6 fusion.54
  212.3 2.6 fusion.54
  215.9 2.6 fusion.54
  219.4 2.6 fusion.54
  223.0 2.6 fusion.54
  226.6 2.6 fusion.54
  230.2 2.6 fusion.54
  233.8 2.6 fusion.54
  237.4 2.6 fusion.54
  241.7 2.0 fusion.10
  243.9 0.8 gather_fusion.2
  244.8 0.8 fusion.41
  245.8 1.4 gather_fusion.1
  247.2 28.3 %reduce-scatter.3.cloned.1.call-done = f32[32,128]{1,0:T(8,128)} async-done(((f32[256,128]{1,0:T(8,128)}), f32[32,128]{1,0:T(8,128)}) %reduce-scatter.3.cloned.1.call-update) | async-done | bytes 16400 | tf_op jit(solution)/shard_map/reduce_scatter | solution.py:138
  276.3 23.8 %all_gather.36 = bf16[32,2048]{1,0:T(8,128)(2,1)S(1)} all-gather(bf16[32,128]{1,0:T(8,128)(2,1)S(1)} %fusion.32), channel_id=1, replica_groups=mesh['tok'=4,'seq'=16,'kv'=2] {'seq'}, dimensions={1}, use_global_device_ids=true | all-gather | bytes 139264 | tf_op jit(solution)/shard_map/all_gather | solution.py:149
  300.3 2.0 convolution_multiply_fusion.4
  302.4 3.2 fusion.13
  305.6 69.0 %reduce-scatter.5.cloned.1.call-done = f32[32,128]{1,0:T(8,128)} async-done(((f32[32,2048]{1,0:T(8,128)}), f32[32,128]{1,0:T(8,128)}) %reduce-scatter.5.cloned.1.call-update) | async-done | bytes 16400 | tf_op jit(solution)/shard_map/reduce_scatter | solution.py:158
  374.6 1.3 add_convert_fusion.2
  (125 shorter events, 25.6 us)
Async XLA Ops:
  6.5 295.8 %copy-start = (bf16[512,2048]{1,0:T(8,128)(2,1)S(1)}, bf16[512,2048]{1,0:T(8,128)(2,1)}, u32[]{:S(2)}) copy-start(bf16[512,2048]{1,0:T(8,128)(2,1)} %param.27) | copy-start | bytes 6291460
  6.5 64.1 %all-gather.6.cloned.1.call-start = ((), (), s32[]{:S(2)}) async-start(), calls=%async_computation.2 | async-start | bytes 1114112 | tf_op jit(solution)/shard_map/all_gather | solution.py:78
  25.3 153.0 %all-gather.8.cloned.1.call-start = ((), (), s32[]{:S(2)}) async-start(), calls=%async_computation.5 | async-start | bytes 8912896 | tf_op jit(solution)/shard_map/all_gather | solution.py:12
  26.1 22.4 %copy-start.7 = (s32[64]{0:T(128)S(1)}, s32[64]{0:T(128)}, u32[]{:S(2)}) copy-start(s32[64]{0:T(128)} %param.17) | copy-start | bytes 772
  78.2 6.2 %copy-start.1 = (pred[64,1024]{1,0:T(8,128)(4,1)S(1)}, pred[64,1024]{1,0:T(8,128)(4,1)}, u32[]{:S(2)}) copy-start(pred[64,1024]{1,0:T(8,128)(4,1)} %broadcast_compare_fusion) | copy-start | bytes 196612
  88.1 6.9 %copy-start.9 = (s32[64]{0:T(128)S(1)}, s32[64]{0:T(128)}, u32[]{:S(2)}) copy-start(s32[64]{0:T(128)} %param.16) | copy-start | bytes 772
  95.0 180.6 %reduce-scatter.3.cloned.1.call-start = ((), (), s32[]{:S(2)}) async-start(), calls=%async_computation.3 | async-start | bytes 147456 | tf_op jit(solution)/shard_map/reduce_scatter | solution.py:138
  95.1 70.7 %copy-start.8 = (pred[4,4]{1,0:T(4,128)(4,1)}, pred[4,4]{1,0:T(4,128)(4,1)S(1)}, u32[]{:S(2)}) copy-start(pred[4,4]{1,0:T(4,128)(4,1)S(1)} %iota_compare_fusion) | copy-start | bytes 52
  127.9 33.5 %copy-start.3 = (bf16[64,4,32]{0,2,1:T(8,128)(2,1)S(1)}, bf16[64,4,32]{0,2,1:T(8,128)(2,1)}, u32[]{:S(2)}) copy-start(bf16[64,4,32]{0,2,1:T(8,128)(2,1)} %get-tuple-element.115) | copy-start | bytes 49156
  127.9 33.5 %copy-start.4 = (bf16[64,4,32]{0,2,1:T(8,128)(2,1)S(1)}, bf16[64,4,32]{0,2,1:T(8,128)(2,1)}, u32[]{:S(2)}) copy-start(bf16[64,4,32]{0,2,1:T(8,128)(2,1)} %get-tuple-element.116) | copy-start | bytes 49156
  178.3 7.7 %slice-start = ((f32[1024,4,4,64]{3,2,1,0:T(4,128)}), f32[64,4,4,64]{3,2,1,0:T(4,128)S(1)}, s32[]{:S(2)}) async-start(f32[1024,4,4,64]{3,2,1,0:T(4,128)} %all-gather.8.cloned.1.call-done), calls=%async_computation.6 | async-start | bytes 1048576 | tf_op jit(solution)/shard_map/slice | solution.py:13
  186.1 55.7 %copy-start.2 = (bf16[64,4,4,4]{3,2,1,0:T(4,128)(2,1)S(1)}, bf16[64,4,4,4]{3,2,1,0:T(4,128)(2,1)}, u32[]{:S(2)}) copy-start(bf16[64,4,4,4]{3,2,1,0:T(4,128)(2,1)} %copy.118) | copy-start | bytes 24580
  241.7 3.1 copy-start.5
  241.7 4.0 %copy-start.6 = (bf16[2048]{0:T(1024)(128)(2,1)S(1)}, bf16[2048]{0:T(1024)(128)(2,1)}, u32[]{:S(2)}) copy-start(bf16[2048]{0:T(1024)(128)(2,1)} %param.24) | copy-start | bytes 12292
  241.7 4.0 %copy-start.10 = (s32[64]{0:T(128)S(1)}, s32[64]{0:T(128)}, u32[]{:S(2)}) copy-start(s32[64]{0:T(128)} %param.16) | copy-start | bytes 772
  245.7 128.9 %reduce-scatter.5.cloned.1.call-start = ((), (), s32[]{:S(2)}) async-start(), calls=%async_computation.4 | async-start | bytes 278528 | tf_op jit(solution)/shard_map/reduce_scatter | solution.py:158
Sparse Core Ops, SparseCore 0:
  25.4 45.2 all-gather.5
  95.1 83.1 all-gather.7
  245.8 29.7 reduce-scatter.2
  305.7 68.8 reduce-scatter.4
